TPU v7x, 32 devices: a whole 2x2x4 slice. The times are simulated.
32 devices in a mesh: tok: 8 (over z, y), head: 4 (over x, core).
Axes of the slice: x: 2, y: 2, z: 4, core: 2. Of those that a mesh axis runs over, the one named last changes fastest.
Arguments:
- queries: bfloat16 [8192, 4096], P(('tok', 'head')), may hold values from -64 to 64
- keys: bfloat16 [8192, 4096], P(('tok', 'head')), may hold values from -6 to 6
- values: bfloat16 [8192, 4096], P(('tok', 'head')), may hold values from -6 to 6
- token_rates: bfloat16 [8192, 8], P(('tok', 'head')), may hold values from 0.099609375 to 1
- gate_start: bfloat16 [8, 512, 1024], P('head'), may hold values from -0.25 to 0.25
- up_start: bfloat16 [8, 512, 1024], P('head'), may hold values from -0.25 to 0.25
- down_start: bfloat16 [8, 1024, 512], P('head'), may hold values from -0.1875 to 0.1875
- norm_gain: float32 [4096], replicated, may hold values from 0.25 to 1.75
- bounds: int32 [4], replicated, may hold values from 896 to 1152
Outputs:
- layer_out: bfloat16 [8192, 4096], P(('tok', 'head'))
Inputs may be any that keep to these rules, and one draw needn't show every extreme that they name: The first span of segment s is its positions below bounds[s].
All inputs are finite; a program needn't handle non-finite values.
Results may differ from a plain program's by a relative error of at most 0.02.
Values may be sent and summed in bfloat16 or wider, within the bound.
A program may use at most 192 MiB of HBM per device.

v0:
```python
import functools
import math
from types import SimpleNamespace

import jax
import jax.numpy as jnp
from jax import lax
from jax.experimental import pallas as pl
from jax.experimental.pallas import tpu as pltpu
from jax.sharding import PartitionSpec as P

AHD = 128
WINDOW = 512
NS_ITERS = 3
CHUNK = 512

linear_coef = 3.4445
cubic_coef = -4.775
quintic_coef = 2.0315
rms_epsilon = 1e-05
norm_epsilon = 1e-06
MESH = pl.DeviceIdType.MESH
F32 = jnp.float32
BF16 = jnp.bfloat16


def mm(a, b, ca=1, cb=0):
    return lax.dot_general(a, b, (((ca,), (cb,)), ((), ())), preferred_element_type=F32)


def logistic(x):
    return 0.5 * jnp.tanh(0.5 * x) + 0.5


def loop(count, fn):
    def step(i, carry):
        fn(i)
        return carry

    lax.fori_loop(0, count, step, 0)


def at(start, size, multiple):
    return pl.ds(pl.multiple_of(start, multiple), size)


def transpose_down(c):
    def step(i):
        cols = at(i * CHUNK, CHUNK, CHUNK)
        c.wdt[:, cols] = c.wd[cols, :].T

    loop(c.hid_width // CHUNK, step)


def transpose_keys(c):
    def step(i):
        c.k_t[:, at(i * 128, 128, 128)] = c.k[at(WINDOW + i * 128, 128, 128), :].T

    loop(c.high // 128, step)


def make_targets(c):
    per_block = c.rows // 128

    def step(i):
        rates = c.rates[i // per_block, 0:1, at((i % per_block) * 128, 128, 128)]
        rate_col = jnp.broadcast_to(rates, (128, 128)).T[:, 0:1]
        values = c.v[at(WINDOW + i * 128, 128, 128), :].astype(F32)
        place = i * 128 + lax.broadcasted_iota(jnp.int32, (128, c.width), 0)
        target = jnp.where(place < c.bound, rate_col * values, 0.0)
        c.target[at(i * 128, 128, 128), :] = target.astype(BF16)
        c.target_t[:, at(i * 128, 128, 128)] = target.T.astype(BF16)

    loop(c.high // 128, step)


def forward(c):
    chunks = c.hid_width // CHUNK

    def step(i):
        rows = at((i // chunks) * c.tile, c.tile, 128)
        cols = at((i % chunks) * CHUNK, CHUNK, CHUNK)
        k_rows = c.k[at(WINDOW + (i // chunks) * c.tile, c.tile, 128), :]
        gate = mm(k_rows, c.wg[:, cols])
        up = mm(k_rows, c.wu[:, cols])
        sig = logistic(gate)
        act = gate * sig
        c.hid[rows, cols] = (act * up).astype(BF16)
        c.act[rows, cols] = act
        c.slope[rows, cols] = up * (sig + act * (1.0 - sig))

    loop((c.high // c.tile) * chunks, step)


def backward(c):
    chunks = c.hid_width // CHUNK

    def step(i):
        rows = at((i // chunks) * c.tile, c.tile, 128)
        cols = at((i % chunks) * CHUNK, CHUNK, CHUNK)
        back = mm(c.target[rows, :], c.wdt[:, cols])
        c.d_gate[rows, cols] = (back * c.slope[rows, cols]).astype(BF16)
        c.d_up[rows, cols] = (back * c.act[rows, cols]).astype(BF16)

    loop((c.high // c.tile) * chunks, step)


def gradients(c):
    def step(i):
        cols = at(i * CHUNK, CHUNK, CHUNK)
        c.grad[0, :, cols] = mm(c.k_t[...], c.d_gate[:, cols])
        c.grad[1, :, cols] = mm(c.k_t[...], c.d_up[:, cols])
        c.grad[2, :, cols] = mm(c.target_t[...], c.hid[:, cols])

    loop(c.hid_width // CHUNK, step)

    def scale(m):
        grad = c.grad[m]
        frob = lax.rsqrt(jnp.sum(grad * grad, keepdims=True) + norm_epsilon)
        c.x[0, m] = (grad * frob).astype(BF16)

    loop(3, scale)


def newton(c):
    def sweep(turn):
        old, new = turn % 2, (turn + 1) % 2
        for m in range(3):
            x = c.x[old, m]
            c.a[m] = mm(x, x, 1, 1).astype(BF16)
        for m in range(3):
            a = c.a[m]
            c.p[m] = (cubic_coef * a.astype(F32) + quintic_coef * mm(a, a)).astype(BF16)
        for m in range(3):
            x = c.x[old, m]
            c.x[new, m] = (linear_coef * x.astype(F32) + mm(c.p[m], x)).astype(BF16)

    loop(NS_ITERS, sweep)


def renorm(c):
    def by_column(i):
        cols = at(i * CHUNK, CHUNK, CHUNK)
        for m, ref in ((0, c.wg), (1, c.wu)):
            w = ref[:, cols].astype(F32)
            u = w + c.x[NS_ITERS % 2, m, :, cols].astype(F32)
            want = jnp.sqrt(jnp.sum(w * w, axis=0, keepdims=True) + norm_epsilon)
            have = jnp.sqrt(jnp.sum(u * u, axis=0, keepdims=True) + norm_epsilon)
            c.x[NS_ITERS % 2, m, :, cols] = (u * (want / have)).astype(BF16)

    loop(c.hid_width // CHUNK, by_column)

    def by_row(i):
        rows = at(i * 128, 128, 128)
        w = c.wdt[rows, :].astype(F32)
        u = w + c.x[NS_ITERS % 2, 2, rows, :].astype(F32)
        want = jnp.sqrt(jnp.sum(w * w, axis=1, keepdims=True) + norm_epsilon)
        have = jnp.sqrt(jnp.sum(u * u, axis=1, keepdims=True) + norm_epsilon)
        c.x[NS_ITERS % 2, 2, rows, :] = (u * (want / have)).astype(BF16)

    loop(c.width // 128, by_row)


def attention(c, first, count):
    tile = WINDOW // 2
    power = math.log2(math.e) / math.sqrt(AHD)

    def step(i):
        t = first + i
        rows = at(t * tile, tile, tile)
        span = at(t * tile, WINDOW + tile, tile)
        below = lax.broadcasted_iota(jnp.int32, (tile, tile), 1) <= lax.broadcasted_iota(
            jnp.int32, (tile, tile), 0
        )
        far_bias = jnp.where(c.first_segment * (2 - t) > 0, F32(-1e30), F32(0.0))
        mid_bias = jnp.where(c.first_segment * (1 - t) > 0, F32(-1e30), F32(0.0))
        for head in range(c.width // AHD):
            feats = slice(head * AHD, (head + 1) * AHD)
            scores = mm(c.q[rows, feats], c.k[span, feats], 1, 1)
            edge = jnp.where(below, scores[:, 2 * tile :], scores[:, :tile] + far_bias)
            mid = scores[:, tile : 2 * tile] + mid_bias
            top = jnp.max(jnp.maximum(edge, mid), axis=1, keepdims=True)
            edge = jnp.exp2((edge - top) * power)
            mid = jnp.exp2((mid - top) * power)
            total = jnp.sum(edge + mid, axis=1, keepdims=True)
            weights = jnp.concatenate(
                [
                    jnp.where(below, 0.0, edge).astype(BF16),
                    mid.astype(BF16),
                    jnp.where(below, edge, 0.0).astype(BF16),
                ],
                axis=1,
            )
            mixed = mm(weights, c.v[span, feats])
            c.out[rows, feats] = (mixed / total).astype(BF16)

    loop(count, step)


def swiglu(c, start, gate, up, down, down_dim):
    q_rows = c.q[at(start, c.rows, c.rows), :]

    def step(i):
        cols = at(i * CHUNK, CHUNK, CHUNK)
        pre_gate = mm(q_rows, gate[:, cols])
        pre_up = mm(q_rows, up[:, cols])
        c.apply_hid[:, cols] = (pre_gate * logistic(pre_gate) * pre_up).astype(BF16)

    loop(c.hid_width // CHUNK, step)
    return mm(c.apply_hid[...], down[...], 1, down_dim)


def fast_rows(c, start):
    new = c.x.at[NS_ITERS % 2]

    @pl.when(start < c.high)
    def _():
        c.raw[...] = swiglu(c, start, c.wg, c.wu, c.wd, 0)

    @pl.when(start + c.rows > c.low)
    def _():
        after = swiglu(c, start, new.at[0], new.at[1], new.at[2], 1)
        place = start + lax.broadcasted_iota(jnp.int32, after.shape, 0)
        kept = (place < c.bound) & (place < c.high)
        c.raw[...] = jnp.where(kept, c.raw[...], after)

    raw = c.raw[...]
    rows = at(start, c.rows, c.rows)
    scale = lax.rsqrt(jnp.mean(raw * raw, axis=1, keepdims=True) + rms_epsilon)
    fast = (raw * scale * c.gain).astype(BF16)
    c.out[rows, :] = (c.out[rows, :].astype(F32) + fast.astype(F32)).astype(BF16)


def scratch_of(length, width, hid_width, rows, peers):
    low, high = length // 2 - length // 16, length // 2 + length // 16
    dma = pltpu.SemaphoreType.DMA
    return {
        "q": pltpu.VMEM((length, width), BF16),
        "k": pltpu.VMEM((WINDOW + length, width), BF16),
        "v": pltpu.VMEM((WINDOW + length, width), BF16),
        "rates": pltpu.VMEM((peers, 8, rows), F32),
        "out": pltpu.VMEM((length, width), BF16),
        "send": dma((4, peers)),
        "recv": dma((4, peers)),
        "own_sem": dma((4,)),
        "halo_send": dma((2,)),
        "halo_recv": dma((2,)),
        "out_send": dma((peers,)),
        "out_recv": dma((peers,)),
        "out_own": dma,
        "wg": pltpu.VMEM((width, hid_width), BF16),
        "wu": pltpu.VMEM((width, hid_width), BF16),
        "wd": pltpu.VMEM((hid_width, width), BF16),
        "wdt": pltpu.VMEM((width, hid_width), BF16),
        "target": pltpu.VMEM((high, width), BF16),
        "target_t": pltpu.VMEM((width, high), BF16),
        "k_t": pltpu.VMEM((width, high), BF16),
        "hid": pltpu.VMEM((high, hid_width), BF16),
        "d_gate": pltpu.VMEM((high, hid_width), BF16),
        "d_up": pltpu.VMEM((high, hid_width), BF16),
        "grad": pltpu.VMEM((3, width, hid_width), F32),
        "x": pltpu.VMEM((2, 3, width, hid_width), BF16),
        "act": pltpu.VMEM((high, hid_width), F32),
        "slope": pltpu.VMEM((high, hid_width), F32),
        "a": pltpu.VMEM((3, width, width), BF16),
        "p": pltpu.VMEM((3, width, width), BF16),
        "apply_hid": pltpu.VMEM((rows, hid_width), BF16),
        "raw": pltpu.VMEM((rows, width), F32),
        "w_sem": dma((3,)),
    }


def sizes(length, width, hid_width, rows):
    low, high = length // 2 - length // 16, length // 2 + length // 16
    return dict(
        length=length, width=width, hid_width=hid_width, rows=rows, low=low, high=high, tile=high // 3
    )


def flip(index, distance, count):
    result, place = 0, 1
    while place < count:
        bit = (index // place) % 2
        result = result + place * (1 - bit if distance & place else bit)
        place *= 2
    return result


def distances(peers):
    return sorted(range(1, peers), key=lambda d: (d > 1, d % 2, d))


def order_of(step, peers):
    half = peers // 2
    return jnp.where(
        step < half - 1, 2 * step + 2, jnp.where(step < peers - 2, 2 * (step - half) + 5, peers - 1 - step)
    )


def flip_by(index, distance, count):
    result, place = 0, 1
    while place < count:
        bit, other = (index // place) % 2, (distance // place) % 2
        result = result + place * (bit + other - 2 * bit * other)
        place *= 2
    return result


def place_of(peer, tok, group):
    return (tok - tok % 2 + peer // group, peer % group)


def feature_of(peer, group):
    return 2 * (peer % group) + peer // group


def greet(others):
    barrier = pltpu.get_barrier_semaphore()
    for other in others:
        pl.semaphore_signal(barrier, inc=1, device_id=other, device_id_type=MESH)
    pl.semaphore_wait(barrier, len(others))


def kernel(
    names, dims, group, toks, bounds, gain, q, k, v, r, gate_all, up_all, down_all, out, *scratch
):
    c = SimpleNamespace(**dims, **dict(zip(names, scratch)))
    tok, column = lax.axis_index("tok"), lax.axis_index("head")
    parity = tok % 2
    peers, rows, width = 2 * group, c.rows, c.width
    me = parity * group + column
    after = ((tok + 2) % toks, column)
    before = ((tok + toks - 2) % toks, column)
    weights = [
        pltpu.make_async_copy(whole.at[parity], mine, c.w_sem.at[i])
        for i, (whole, mine) in enumerate(((gate_all, c.wg), (up_all, c.wu), (down_all, c.wd)))
    ]
    for copy in weights:
        copy.start()
    c.gain = gain[2 * column + parity]
    c.bound = bounds[tok // 2]
    c.first_segment = jnp.where(tok < 2, 1, 0)
    greet([place_of(flip(me, d, peers), tok, group) for d in range(1, peers)] + [after, before])

    def source(t, peer):
        j = feature_of(peer, group)
        if t == 3:
            return r.at[j]
        return (k, v, q)[t].at[:, at(j * width, width, width)]

    def slot(t, peer):
        if t == 3:
            return c.rates.at[peer]
        shift = WINDOW if t < 2 else 0
        return (c.k, c.v, c.q)[t].at[at(shift + peer * rows, rows, rows), :]

    def remote(t, peer):
        return pltpu.make_async_remote_copy(
            source(t, peer), slot(t, me), c.send.at[t, peer], c.recv.at[t, me],
            device_id=place_of(peer, tok, group), device_id_type=MESH,
        )

    def own(t):
        return pltpu.make_async_copy(source(t, me), slot(t, me), c.own_sem.at[t])

    def arrived(t, peer):
        @pl.when(me != peer)
        def _():
            pltpu.make_async_remote_copy(
                slot(t, peer), slot(t, peer), c.send.at[t, peer], c.recv.at[t, peer],
                device_id=place_of(peer, tok, group), device_id_type=MESH,
            ).wait_recv()

        @pl.when(me == peer)
        def _():
            own(t).wait()

    def block(peer):
        return out.at[:, at(feature_of(peer, group) * width, width, width)]

    def done_rows(peer):
        return c.out.at[at(peer * rows, rows, rows), :]

    def give(peer):
        return pltpu.make_async_remote_copy(
            done_rows(peer), block(me), c.out_send.at[peer], c.out_recv.at[me],
            device_id=place_of(peer, tok, group), device_id_type=MESH,
        )

    def taken(peer):
        return pltpu.make_async_remote_copy(
            done_rows(peer), block(peer), c.out_send.at[peer], c.out_recv.at[peer],
            device_id=place_of(peer, tok, group), device_id_type=MESH,
        )

    order = distances(peers)
    for t in (3, 0):
        for d in order:
            remote(t, flip(me, d, peers)).start()
        own(t).start()

    halos = [
        pltpu.make_async_remote_copy(
            o.at[pl.ds(c.length, WINDOW), :], o.at[pl.ds(0, WINDOW), :],
            c.halo_send.at[t], c.halo_recv.at[t], device_id=after, device_id_type=MESH,
        )
        for t, o in enumerate((c.k, c.v))
    ]

    def send_next(t):
        for d in order:
            remote(t - 1, flip(me, d, peers)).wait_send()
            remote(t, flip(me, d, peers)).start()
        own(t).start()

    for copy in weights:
        copy.wait()
    transpose_down(c)
    send_next(1)
    needed = -(-c.high // rows)
    for p in range(needed):
        arrived(0, p)
    for p in range(needed, peers):
        arrived(0, p)
    halos[0].start()
    forward(c)
    transpose_keys(c)
    send_next(2)
    for p in range(peers):
        arrived(3, p)
    for p in range(needed):
        arrived(1, p)
    for p in range(needed, peers):
        arrived(1, p)
    halos[1].start()
    make_targets(c)
    backward(c)
    gradients(c)
    newton(c)
    renorm(c)
    for halo in halos:
        halo.wait()
    tiles = rows // (WINDOW // 2)

    def turn(step):
        peer = flip_by(me, jnp.where(step == 0, 0, order_of(step - 1, peers)), peers)
        arrived(2, peer)
        attention(c, peer * tiles, tiles)
        fast_rows(c, peer * rows)

        @pl.when(peer != me)
        def _():
            give(peer).start()

        @pl.when(peer == me)
        def _():
            pltpu.make_async_copy(done_rows(me), block(me), c.out_own).start()

    loop(peers, turn)
    pltpu.make_async_copy(done_rows(me), block(me), c.out_own).wait()
    for d in order:
        taken(flip(me, d, peers)).wait_recv()
    for d in order:
        give(flip(me, d, peers)).wait_send()
        for t in (2, 3):
            remote(t, flip(me, d, peers)).wait_send()


def body(queries, keys, values, token_rates, gate_start, up_start, down_start, norm_gain, bounds):
    rows, feats = queries.shape
    group, toks = lax.axis_size("head"), lax.axis_size("tok")
    heads, width, hid_width = token_rates.shape[1], gate_start.shape[1], gate_start.shape[2]
    peers = 2 * group
    length = peers * rows
    anywhere = pl.BlockSpec(memory_space=pl.ANY)
    vmem = pl.BlockSpec(memory_space=pltpu.VMEM)
    dma = pltpu.SemaphoreType.DMA
    rates = jnp.broadcast_to(token_rates.T.astype(F32)[:, None, :], (heads, 8, rows))
    scratch = scratch_of(length, width, hid_width, rows, peers)
    return pl.pallas_call(
        functools.partial(
            kernel, tuple(scratch), sizes(length, width, hid_width, rows), group, toks
        ),
        out_shape=jax.ShapeDtypeStruct((rows, feats), BF16),
        in_specs=[pl.BlockSpec(memory_space=pltpu.SMEM), vmem] + [anywhere] * 7,
        out_specs=anywhere,
        scratch_shapes=list(scratch.values()),
        compiler_params=pltpu.CompilerParams(
            collective_id=0, has_side_effects=True, vmem_limit_bytes=66000000
        ),
        name="layer",
    )(
        bounds, norm_gain.reshape(heads, 1, width), queries, keys, values, rates,
        gate_start, up_start, down_start,
    )


def solution(mesh):
    spread = P(("tok", "head"), None)
    owned = P("head", None, None)
    return jax.shard_map(
        body,
        mesh=mesh,
        in_specs=(spread,) * 4 + (owned,) * 3 + (P(), P()),
        out_specs=spread,
        check_vma=False,
    )
```

profile of v0, /device:TPU:0, one launch (start us, length us, event | category | flops | bytes accessed | tf_op | source)
XLA Modules:
  0.0 123.8 jit_solution(3100384352171752128)
XLA Ops:
  0.0 0.7 convert_bitcast_fusion
  0.7 0.6 broadcast_in_dim.2.r
  1.3 119.3 %layer.1 = bf16[256,4096]{1,0:T(8,128)(2,1)} custom-call(s32[4]{0:T(128)} %bounds.1, f32[8,1,512]{2,1,0:T(1,128)} %bitcast.3, bf16[256,4096]{1,0:T(8,128)(2,1)} %q.1, bf16[256,4096]{1,0:T(8,128)(2,1)} %k.1, bf16[256,4096]{1,0:T(8,128)(2,1)} %v.1, f32[8,8,256]{2,1,0:T(8,128)} %broadcast_in_dim.2.r, bf16[2,512,1024]{2,1,0:T(8,128)(2,1)} %gate_all.1, ...), custom_call_target="tpu_custom_call" | custom-call | tf_op jit(solution)/shard_map/layer/pallas_call | solution.py:480
  120.7 3.1 %copy.11 = bf16[256,4096]{1,0:T(8,128)(2,1)} copy(bf16[256,4096]{1,0:T(8,128)(2,1)} %layer.1) | data formatting | bytes 4194304
where the time goes:
time: 124 us
  Pallas kernels  119 us (96%)
  local copies, waits for them, and re-layouts  3.77 us (3%)
    pallas_call x1, Pallas kernels, body(): pl.pallas_call(functools.partial(kernel, tuple(scratch), sizes(length, wi...  119 us
    unnamed x1, local copies, waits for them, and re-layouts  3.13 us

commit v1 on v0

v1 whole, which is shorter than its diff:
```python
import functools
import math
from types import SimpleNamespace

import jax
import jax.numpy as jnp
from jax import lax
from jax.experimental import pallas as pl
from jax.experimental.pallas import tpu as pltpu
from jax.sharding import PartitionSpec as P

AHD = 128
WINDOW = 512
NS_ITERS = 3
CHUNK = 512

linear_coef = 3.4445
cubic_coef = -4.775
quintic_coef = 2.0315
rms_epsilon = 1e-05
norm_epsilon = 1e-06
MESH = pl.DeviceIdType.MESH
F32 = jnp.float32
BF16 = jnp.bfloat16


def mm(a, b, ca=1, cb=0):
    return lax.dot_general(a, b, (((ca,), (cb,)), ((), ())), preferred_element_type=F32)


def logistic(x):
    return 0.5 * jnp.tanh(0.5 * x) + 0.5


def loop(count, fn):
    def step(i, carry):
        fn(i)
        return carry

    lax.fori_loop(0, count, step, 0)


def at(start, size, multiple):
    return pl.ds(pl.multiple_of(start, multiple), size)


def transpose_down(c):
    def step(i):
        cols = at(i * CHUNK, CHUNK, CHUNK)
        c.wdt[:, cols] = c.wd[cols, :].T

    loop(c.hid_width // CHUNK, step)


def clear_gradients(c):
    def step(i):
        c.grad[:, at(i * 64, 64, 64), :] = jnp.zeros((3, 64, c.hid_width), F32)

    loop(c.width // 64, step)


def train_rows(c, block, start, size):
    for i in range(size // 128):
        part = slice(i * 128, (i + 1) * 128)
        here = at(WINDOW + start + i * 128, 128, 128)
        rates = c.rates[block, :, part].astype(F32)
        mine = lax.broadcasted_iota(jnp.int32, rates.shape, 0) == c.feature
        rates = jnp.sum(jnp.where(mine, rates, 0.0), axis=0, keepdims=True)
        rate_col = jnp.broadcast_to(rates, (128, 128)).T[:, 0:1]
        place = start + i * 128 + lax.broadcasted_iota(jnp.int32, (128, c.width), 0)
        target = jnp.where(place < c.bound, rate_col * c.v[here, :].astype(F32), 0.0)
        c.target[part, :] = target.astype(BF16)
        c.target_t[:, part] = target.T.astype(BF16)
        c.k_t[:, part] = c.k[here, :].T
    k_rows = c.k[at(WINDOW + start, size, 128), :]
    for i in range(c.hid_width // CHUNK):
        cols = slice(i * CHUNK, (i + 1) * CHUNK)
        gate = mm(k_rows, c.wg[:, cols])
        up = mm(k_rows, c.wu[:, cols])
        sig = logistic(gate)
        act = gate * sig
        slope = up * (sig + act * (1.0 - sig))
        back = mm(c.target[:size, :], c.wdt[:, cols])
        lefts = (c.k_t, c.k_t, c.target_t)
        rights = (back * slope, back * act, act * up)
        for m, (left, right) in enumerate(zip(lefts, rights)):
            c.grad[m, :, cols] += mm(left[:, :size], right.astype(BF16))


def scale_gradients(c):
    def scale(m):
        grad = c.grad[m]
        frob = lax.rsqrt(jnp.sum(grad * grad, keepdims=True) + norm_epsilon)
        c.x[0, m] = (grad * frob).astype(BF16)

    loop(3, scale)


def sweep(c, turn):
    old, new = turn % 2, (turn + 1) % 2
    for m in range(3):
        x = c.x[old, m]
        c.a[m] = mm(x, x, 1, 1).astype(BF16)
    for m in range(3):
        a = c.a[m]
        c.p[m] = (cubic_coef * a.astype(F32) + quintic_coef * mm(a, a)).astype(BF16)
    for m in range(3):
        x = c.x[old, m]
        c.x[new, m] = (linear_coef * x.astype(F32) + mm(c.p[m], x)).astype(BF16)


def renorm(c):
    def by_column(i):
        cols = at(i * CHUNK, CHUNK, CHUNK)
        for m, ref in ((0, c.wg), (1, c.wu)):
            w = ref[:, cols].astype(F32)
            u = w + c.x[NS_ITERS % 2, m, :, cols].astype(F32)
            want = jnp.sqrt(jnp.sum(w * w, axis=0, keepdims=True) + norm_epsilon)
            have = jnp.sqrt(jnp.sum(u * u, axis=0, keepdims=True) + norm_epsilon)
            c.x[NS_ITERS % 2, m, :, cols] = (u * (want / have)).astype(BF16)

    loop(c.hid_width // CHUNK, by_column)

    def by_row(i):
        rows = at(i * 128, 128, 128)
        w = c.wdt[rows, :].astype(F32)
        u = w + c.x[NS_ITERS % 2, 2, rows, :].astype(F32)
        want = jnp.sqrt(jnp.sum(w * w, axis=1, keepdims=True) + norm_epsilon)
        have = jnp.sqrt(jnp.sum(u * u, axis=1, keepdims=True) + norm_epsilon)
        c.x[NS_ITERS % 2, 2, rows, :] = (u * (want / have)).astype(BF16)

    loop(c.width // 128, by_row)


def attention(c, first, count):
    tile = WINDOW // 2
    power = math.log2(math.e) / math.sqrt(AHD)

    def step(i):
        t = first + i
        rows = at(t * tile, tile, tile)
        span = at(t * tile, WINDOW + tile, tile)
        below = lax.broadcasted_iota(jnp.int32, (tile, tile), 1) <= lax.broadcasted_iota(
            jnp.int32, (tile, tile), 0
        )
        far_bias = jnp.where(c.first_segment * (2 - t) > 0, F32(-1e30), F32(0.0))
        mid_bias = jnp.where(c.first_segment * (1 - t) > 0, F32(-1e30), F32(0.0))
        for head in range(c.width // AHD):
            feats = slice(head * AHD, (head + 1) * AHD)
            scores = mm(c.q[rows, feats], c.k[span, feats], 1, 1)
            edge = jnp.where(below, scores[:, 2 * tile :], scores[:, :tile] + far_bias)
            mid = scores[:, tile : 2 * tile] + mid_bias
            top = jnp.max(jnp.maximum(edge, mid), axis=1, keepdims=True)
            edge = jnp.exp2((edge - top) * power)
            mid = jnp.exp2((mid - top) * power)
            total = jnp.sum(edge + mid, axis=1, keepdims=True)
            weights = jnp.concatenate(
                [
                    jnp.where(below, 0.0, edge).astype(BF16),
                    mid.astype(BF16),
                    jnp.where(below, edge, 0.0).astype(BF16),
                ],
                axis=1,
            )
            mixed = mm(weights, c.v[span, feats])
            c.out[rows, feats] = (mixed / total).astype(BF16)

    loop(count, step)


def swiglu(c, start, size, gate, up, down, down_dim):
    q_rows = c.q[at(start, size, 128), :]
    for i in range(c.hid_width // CHUNK):
        cols = slice(i * CHUNK, (i + 1) * CHUNK)
        pre_gate = mm(q_rows, gate[:, cols])
        pre_up = mm(q_rows, up[:, cols])
        c.apply_hid[:size, cols] = (pre_gate * logistic(pre_gate) * pre_up).astype(BF16)
    return mm(c.apply_hid[:size, :], down[...], 1, down_dim)


def old_rows(c, start, size):
    return swiglu(c, start, size, c.wg, c.wu, c.wd, 0)


def new_rows(c, start, size):
    new = c.x.at[NS_ITERS % 2]
    return swiglu(c, start, size, new.at[0], new.at[1], new.at[2], 1)


def finish_rows(c, start, raw):
    rows = at(start, raw.shape[0], 128)
    scale = lax.rsqrt(jnp.mean(raw * raw, axis=1, keepdims=True) + rms_epsilon)
    fast = (raw * scale * c.gain[c.feature]).astype(BF16)
    c.out[rows, :] = (c.out[rows, :].astype(F32) + fast.astype(F32)).astype(BF16)


def below_bound(c, start, shape):
    return start + lax.broadcasted_iota(jnp.int32, shape, 0) < c.bound


def fast_old(c, quarter):
    size, edge = c.quarter, c.high - c.low
    edge //= 2
    start = quarter * size
    c.raw[...] = old_rows(c, start, size)
    finish_rows(c, start, c.raw[: size - edge, :])

    @pl.when(quarter == 0)
    def _():
        finish_rows(c, start + size - edge, c.raw[size - edge :, :])

    @pl.when(quarter == 1)
    def _():
        c.open_raw[...] = c.raw[size - edge :, :]


def close_edge(c):
    edge = (c.high - c.low) // 2
    after = new_rows(c, c.low, edge)
    finish_rows(c, c.low, jnp.where(below_bound(c, c.low, after.shape), c.open_raw[...], after))


def fast_new(c, quarter):
    size, edge = c.quarter, (c.high - c.low) // 2
    start = quarter * size
    c.raw[...] = new_rows(c, start, size)

    @pl.when(quarter == 2)
    def _():
        before = old_rows(c, start, edge)
        after = c.raw[:edge, :]
        c.raw[:edge, :] = jnp.where(below_bound(c, start, after.shape), before, after)

    finish_rows(c, start, c.raw[...])


def scratch_of(length, width, hid_width, rows, peers):
    dma = pltpu.SemaphoreType.DMA
    quarter, edge = length // 4, length // 16
    return {
        "q": pltpu.VMEM((length, width), BF16),
        "k": pltpu.VMEM((WINDOW + length, width), BF16),
        "v": pltpu.VMEM((WINDOW + length, width), BF16),
        "my_rates": pltpu.VMEM((peers, rows), BF16),
        "rates": pltpu.VMEM((peers, peers, rows), BF16),
        "gain": pltpu.VMEM((peers, 1, width), F32),
        "out": pltpu.VMEM((length, width), BF16),
        "kv_send": dma((2, 2, peers)),
        "kv_recv": dma((2, 2, peers)),
        "q_send": dma((peers,)),
        "q_recv": dma((peers,)),
        "rate_send": dma((peers,)),
        "rate_recv": dma((peers,)),
        "own_sem": dma((3,)),
        "halo_send": dma((2,)),
        "halo_recv": dma((2,)),
        "out_send": dma((peers,)),
        "out_recv": dma((peers,)),
        "out_own": dma,
        "wg": pltpu.VMEM((width, hid_width), BF16),
        "wu": pltpu.VMEM((width, hid_width), BF16),
        "wd": pltpu.VMEM((hid_width, width), BF16),
        "wdt": pltpu.VMEM((width, hid_width), BF16),
        "target": pltpu.VMEM((rows, width), BF16),
        "target_t": pltpu.VMEM((width, rows), BF16),
        "k_t": pltpu.VMEM((width, rows), BF16),
        "grad": pltpu.VMEM((3, width, hid_width), F32),
        "x": pltpu.VMEM((2, 3, width, hid_width), BF16),
        "a": pltpu.VMEM((3, width, width), BF16),
        "p": pltpu.VMEM((3, width, width), BF16),
        "apply_hid": pltpu.VMEM((quarter, hid_width), BF16),
        "raw": pltpu.VMEM((quarter, width), F32),
        "open_raw": pltpu.VMEM((edge, width), F32),
        "w_sem": dma((5,)),
    }


def sizes(length, width, hid_width, rows):
    low, high = length // 2 - length // 16, length // 2 + length // 16
    return dict(
        length=length, width=width, hid_width=hid_width, rows=rows, low=low, high=high, quarter=length // 4
    )


def flip(index, distance, count):
    result, place = 0, 1
    while place < count:
        bit = (index // place) % 2
        result = result + place * (1 - bit if distance & place else bit)
        place *= 2
    return result


def flip_by(index, distance, count):
    result, place = 0, 1
    while place < count:
        bit, other = (index // place) % 2, (distance // place) % 2
        result = result + place * (bit + other - 2 * bit * other)
        place *= 2
    return result


def place_of(peer, tok, group):
    return (tok - tok % 2 + peer // group, peer % group)


def feature_of(peer, group):
    return 2 * (peer % group) + peer // group


def greet(others, neighbours, meanwhile):
    barrier = pltpu.get_barrier_semaphore()
    count = len(others)
    for other in others:
        pl.semaphore_signal(barrier, inc=1, device_id=other, device_id_type=MESH)
    for exists, other in neighbours:
        count = count + jnp.where(exists, 1, 0)

        @pl.when(exists)
        def _(other=other):
            pl.semaphore_signal(barrier, inc=1, device_id=other, device_id_type=MESH)

    meanwhile()
    pl.semaphore_wait(barrier, count)


def pick(index, values):
    result = values[-1]
    for i, value in enumerate(values[:-1]):
        result = jnp.where(index == i, value, result)
    return result


def kernel(
    names, dims, group, toks, bounds, gain, q, k, v, r, gate_all, up_all, down_all, out, *scratch
):
    c = SimpleNamespace(**dims, **dict(zip(names, scratch)))
    tok, column = lax.axis_index("tok"), lax.axis_index("head")
    parity = tok % 2
    peers, rows, width = 2 * group, c.rows, c.width
    half, part = group // 2, rows // 2
    side = column // half
    me = parity * group + column
    first_late = group
    after = ((tok + 2) % toks, column)
    before = ((tok + toks - 2) % toks, column)
    has_after, has_before = tok < toks - 2, tok >= 2
    c.feature = 2 * column + parity
    c.bound = bounds[tok // 2]
    c.first_segment = jnp.where(tok < 2, 1, 0)
    loads = [
        pltpu.make_async_copy(source, mine, c.w_sem.at[i])
        for i, (source, mine) in enumerate(
            (
                (r, c.my_rates),
                (gain, c.gain),
                (gate_all.at[parity], c.wg),
                (up_all.at[parity], c.wu),
                (down_all.at[parity], c.wd),
            )
        )
    ]

    def columns(peer):
        return at(feature_of(peer, group) * width, width, width)

    def slot(t, start, size):
        return (c.k, c.v, c.q)[t].at[at((WINDOW if t < 2 else 0) + start, size, 128), :]

    owns = [
        pltpu.make_async_copy((k, v, q)[t].at[:, columns(me)], slot(t, me * rows, rows), c.own_sem.at[t])
        for t in range(3)
    ]

    def load():
        for copy in loads + owns:
            copy.start()
        loads[0].wait()
        c.rates[me] = c.my_rates[...]

    everybody = [place_of(flip(me, d, peers), tok, group) for d in range(1, peers)]
    greet(everybody, ((has_after, after), (has_before, before)), load)

    def remote(source, target, send, recv, peer):
        return pltpu.make_async_remote_copy(
            source, target, send, recv, device_id=place_of(peer, tok, group), device_id_type=MESH
        )

    def kv_copy(t, h, peer):
        return remote(
            (k, v)[t].at[pl.ds(h * part, part), columns(peer)],
            slot(t, me * rows + h * part, part),
            c.kv_send.at[t, h, peer], c.kv_recv.at[t, h, me], peer,
        )

    def q_copy(peer):
        return remote(
            q.at[:, columns(peer)], slot(2, me * rows, rows), c.q_send.at[peer], c.q_recv.at[me], peer
        )

    def rate_copy(peer):
        return remote(c.my_rates, c.rates.at[me], c.rate_send.at[peer], c.rate_recv.at[me], peer)

    def got_kv(peer, h):
        @pl.when(me != peer)
        def _():
            for t in range(2):
                target = slot(t, peer * rows + h * part, part)
                remote(target, target, c.kv_send.at[t, h, peer], c.kv_recv.at[t, h, peer], peer).wait_recv()

    def got_q(peer):
        @pl.when(me != peer)
        def _():
            target = slot(2, peer * rows, rows)
            remote(target, target, c.q_send.at[peer], c.q_recv.at[peer], peer).wait_recv()

    def got_rates(peer):
        @pl.when(me != peer)
        def _():
            target = c.rates.at[peer]
            remote(target, target, c.rate_send.at[peer], c.rate_recv.at[peer], peer).wait_recv()

    def block(peer):
        return out.at[:, columns(peer)]

    def done_rows(peer):
        return c.out.at[at(peer * rows, rows, rows), :]

    def give(peer):
        return remote(done_rows(peer), block(me), c.out_send.at[peer], c.out_recv.at[me], peer)

    def taken(peer):
        return remote(done_rows(peer), block(peer), c.out_send.at[peer], c.out_recv.at[peer], peer)

    keep = pltpu.make_async_copy(done_rows(me), block(me), c.out_own)

    def hand_out(peer):
        @pl.when(peer != me)
        def _():
            give(peer).start()

        @pl.when(peer == me)
        def _():
            keep.start()

    halos = [
        pltpu.make_async_remote_copy(
            o.at[pl.ds(c.length, WINDOW), :], o.at[pl.ds(0, WINDOW), :],
            c.halo_send.at[t], c.halo_recv.at[t], device_id=after, device_id_type=MESH,
        )
        for t, o in enumerate((c.k, c.v))
    ]

    chip = list(range(1, half))
    along = list(range(half, group))
    across = list(range(group, group + half))
    corner = list(range(group + half, peers))
    near = [d for pair in zip(along, across) for d in pair]
    everyone = chip + near + corner

    def send_kv(ds, hs=(0, 1), owner=True):
        for d in ds:
            for h in hs:
                def start():
                    for t in range(2):
                        kv_copy(t, h, flip(me, d, peers)).start()

                if h == 0 and owner:
                    pl.when(me != first_late)(start)
                else:
                    start()

    def send_q(ds):
        for d in ds:
            q_copy(flip(me, d, peers)).start()

    has_rates = (parity == 0) | (me == first_late)

    @pl.when(has_rates)
    def _():
        for d in everyone:
            rate_copy(flip(me, d, peers)).start()

    @pl.when(me == first_late)
    def _():
        send_kv(corner + near + chip, (0,), False)

    send_kv(chip + near)
    send_q(chip)

    @pl.when(parity == 1)
    def _():
        send_q(near)

    def send_corner():
        send_kv(corner)
        send_q(corner)

    pl.when((parity == 0) | (side == 0))(send_corner)

    @pl.when(parity == 0)
    def _():
        send_q(along)

    for copy in loads[1:] + owns:
        copy.wait()
    transpose_down(c)
    clear_gradients(c)

    @pl.when(tok < 2)
    def _():
        c.k[:WINDOW, :] = jnp.zeros((WINDOW, width), BF16)
        c.v[:WINDOW, :] = jnp.zeros((WINDOW, width), BF16)

    tiles = c.quarter // (WINDOW // 2)

    def got_first_late():
        got_kv(first_late, 1)
        for p in range(group + 1, group + half):
            for h in range(2):
                got_kv(p, h)

    def got_last():
        for p in range(group + half, peers):
            for h in range(2):
                got_kv(p, h)
        for halo in halos:
            pl.when(has_after)(halo.start)

    def attend(quarter):
        for j in range(half):
            got_q(quarter * half + j)

        @pl.when(quarter == 0)
        def _():
            for halo in halos:
                pl.when(has_before)(halo.wait_recv)

        attention(c, quarter * tiles, tiles)

    def train(i):
        p = flip_by(column, i, group)
        got_rates(p)
        for h in range(2):
            got_kv(p, h)
        train_rows(c, p, p * rows, rows)

        @pl.when(i == half - 1)
        def _():
            got_rates(first_late)
            got_kv(first_late, 0)
            train_rows(c, first_late, c.length // 2, part)

            @pl.when(parity == 1)
            def _():
                got_first_late()
                got_last()
                attend(3)

                @pl.when(side == 1)
                def _():
                    got_q(2 * half)
                    send_corner()
                    got_q(2 * half + 1)
                    attention(c, 2 * tiles, tiles)

    loop(group, train)

    @pl.when((parity == 0) & (side == 0))
    def _():
        got_first_late()

    @pl.when((parity == 0) & (side == 1))
    def _():
        got_last()

    scale_gradients(c)

    def improve(i):
        sweep(c, i)
        quarter = 1 - side

        @pl.when((parity == 1) & (i == 0))
        def _():
            attend(quarter)
            fast_old(c, quarter)
            for j in range(half):
                pl.when((quarter == 0) | (j < half - 1))(
                    functools.partial(hand_out, quarter * half + j)
                )

    loop(NS_ITERS, improve)
    renorm(c)

    def last(s):
        early = jnp.where(side == 0, pick(s, (2, 1, 3, 0)), pick(s, (1, 3, 0, 2)))
        late = pick(s, (3 - side, side, 2 + side))
        quarter = jnp.where(parity == 0, early, late)

        @pl.when((parity == 0) & (s == 1))
        def _():
            pl.when(side == 0)(got_last)
            pl.when(side == 1)(got_first_late)

        @pl.when((parity == 0) | (s == 1) | ((s == 2) & (side == 0)))
        def _():
            attend(quarter)

        @pl.when(quarter < 2)
        def _():
            fast_old(c, quarter)

        @pl.when(quarter >= 2)
        def _():
            fast_new(c, quarter)

        for j in range(half):
            pl.when((quarter != 1) | (j < half - 1))(
                functools.partial(hand_out, quarter * half + j)
            )

        @pl.when((quarter == 1) | ((parity == 1) & (side == 0) & (s == 0)))
        def _():
            close_edge(c)
            hand_out(group - 1)

        @pl.when((parity == 0) & (s == 0))
        def _():
            send_q(across)

    loop(jnp.where(parity == 0, 4, 3), last)
    keep.wait()
    for d in everyone:
        taken(flip(me, d, peers)).wait_recv()
    for d in everyone:
        peer = flip(me, d, peers)
        give(peer).wait_send()
        q_copy(peer).wait_send()
        for t in range(2):
            for h in range(2):
                kv_copy(t, h, peer).wait_send()
    for halo in halos:
        pl.when(has_after)(halo.wait_send)

    @pl.when(has_rates)
    def _():
        for d in everyone:
            rate_copy(flip(me, d, peers)).wait_send()


def body(queries, keys, values, token_rates, gate_start, up_start, down_start, norm_gain, bounds):
    rows, feats = queries.shape
    group, toks = lax.axis_size("head"), lax.axis_size("tok")
    heads, width, hid_width = token_rates.shape[1], gate_start.shape[1], gate_start.shape[2]
    peers = 2 * group
    length = peers * rows
    anywhere = pl.BlockSpec(memory_space=pl.ANY)
    scratch = scratch_of(length, width, hid_width, rows, peers)
    return pl.pallas_call(
        functools.partial(
            kernel, tuple(scratch), sizes(length, width, hid_width, rows), group, toks
        ),
        out_shape=jax.ShapeDtypeStruct((rows, feats), BF16),
        in_specs=[pl.BlockSpec(memory_space=pltpu.SMEM)] + [anywhere] * 8,
        out_specs=anywhere,
        scratch_shapes=list(scratch.values()),
        compiler_params=pltpu.CompilerParams(
            collective_id=0, has_side_effects=True, vmem_limit_bytes=66000000
        ),
        name="layer",
    )(
        bounds, norm_gain.reshape(heads, 1, width), queries, keys, values, token_rates.T,
        gate_start, up_start, down_start,
    )


def solution(mesh):
    spread = P(("tok", "head"), None)
    owned = P("head", None, None)
    return jax.shard_map(
        body,
        mesh=mesh,
        in_specs=(spread,) * 4 + (owned,) * 3 + (P(), P()),
        out_specs=spread,
        check_vma=False,
    )
```

time: 124 us -> 112 us (0.903)
  the two profiles are of different devices: /device:TPU:0 before, /device:TPU:27 now
where the time goes in v1:
time: 112 us
  Pallas kernels  108 us (96%)
  local copies, waits for them, and re-layouts  3.13 us (3%)
    pallas_call x1, Pallas kernels, body(): pl.pallas_call(functools.partial(kernel, tuple(scratch), sizes(length, wi...  108 us
    unnamed x1, local copies, waits for them, and re-layouts  3.13 us

profile of v1, /device:TPU:27, one launch (start us, length us, event | category | flops | bytes accessed | tf_op | source)
XLA Modules:
  0.0 111.5 jit_solution(114903929822862686)
XLA Ops:
  0.0 108.4 %layer.1 = bf16[256,4096]{1,0:T(8,128)(2,1)} custom-call(s32[4]{0:T(128)} %bounds.1, f32[8,1,512]{2,1,0:T(1,128)} %bitcast.2, bf16[256,4096]{1,0:T(8,128)(2,1)} %q.1, bf16[256,4096]{1,0:T(8,128)(2,1)} %k.1, bf16[256,4096]{1,0:T(8,128)(2,1)} %v.1, bf16[8,256]{1,0:T(8,128)(2,1)} %bitcast.3, bf16[2,512,1024]{2,1,0:T(8,128)(2,1)} %gate_all.1, ...), custom_call_target="tpu_custom_call" | custom-call | tf_op jit(solution)/shard_map/layer/pallas_call | solution.py:659
  108.4 3.1 %copy.11 = bf16[256,4096]{1,0:T(8,128)(2,1)} copy(bf16[256,4096]{1,0:T(8,128)(2,1)} %layer.1) | data formatting | bytes 4194304

commit v2 on v1

--- a/solution.py
+++ b/solution.py
@@ -84,52 +84,67 @@
         lefts = (c.k_t, c.k_t, c.target_t)
         rights = (back * slope, back * act, act * up)
         for m, (left, right) in enumerate(zip(lefts, rights)):
-            c.grad[m, :, cols] += mm(left[:, :size], right.astype(BF16))
+            total = c.grad[m, :, cols] + mm(left[:, :size], right.astype(BF16))
+            c.grad[m, :, cols] = total
+            c.squares[m, :, cols] = jnp.sum((total * total).reshape(-1, 8, CHUNK), axis=0)
 
 
 def scale_gradients(c):
-    def scale(m):
-        grad = c.grad[m]
-        frob = lax.rsqrt(jnp.sum(grad * grad, keepdims=True) + norm_epsilon)
-        c.x[0, m] = (grad * frob).astype(BF16)
-
-    loop(3, scale)
+    for m in range(3):
+        frob = lax.rsqrt(jnp.sum(c.squares[m], keepdims=True) + norm_epsilon)
+        c.x[0, m] = (c.grad[m] * frob).astype(BF16)
+
+
+def symmetric(ref, m, size, top, corner):
+    ref[m, :size, :] = top
+    ref[m, size:, size:] = corner
+    ref[m, size:, :size] = top[:, size:].T
 
 
 def sweep(c, turn):
-    old, new = turn % 2, (turn + 1) % 2
+    old, new, h = turn % 2, (turn + 1) % 2, c.width // 2
     for m in range(3):
         x = c.x[old, m]
-        c.a[m] = mm(x, x, 1, 1).astype(BF16)
+        top, corner = mm(x[:h], x, 1, 1), mm(x[h:], x[h:], 1, 1)
+        symmetric(c.a, m, h, top.astype(BF16), corner.astype(BF16))
     for m in range(3):
         a = c.a[m]
-        c.p[m] = (cubic_coef * a.astype(F32) + quintic_coef * mm(a, a)).astype(BF16)
+        top = cubic_coef * a[:h].astype(F32) + quintic_coef * mm(a[:h], a)
+        corner = cubic_coef * a[h:, h:].astype(F32) + quintic_coef * mm(a[h:], a[:, h:])
+        symmetric(c.p, m, h, top.astype(BF16), corner.astype(BF16))
     for m in range(3):
         x = c.x[old, m]
         c.x[new, m] = (linear_coef * x.astype(F32) + mm(c.p[m], x)).astype(BF16)
 
 
-def renorm(c):
-    def by_column(i):
-        cols = at(i * CHUNK, CHUNK, CHUNK)
-        for m, ref in ((0, c.wg), (1, c.wu)):
+def measure_start(c):
+    for m, ref in ((0, c.wg), (1, c.wu)):
+        for i in range(c.hid_width // CHUNK):
+            cols = slice(i * CHUNK, (i + 1) * CHUNK)
             w = ref[:, cols].astype(F32)
-            u = w + c.x[NS_ITERS % 2, m, :, cols].astype(F32)
-            want = jnp.sqrt(jnp.sum(w * w, axis=0, keepdims=True) + norm_epsilon)
-            have = jnp.sqrt(jnp.sum(u * u, axis=0, keepdims=True) + norm_epsilon)
-            c.x[NS_ITERS % 2, m, :, cols] = (u * (want / have)).astype(BF16)
-
-    loop(c.hid_width // CHUNK, by_column)
+            c.want[m, :, cols] = jnp.sqrt(jnp.sum(w * w, axis=0, keepdims=True) + norm_epsilon)
 
     def by_row(i):
         rows = at(i * 128, 128, 128)
         w = c.wdt[rows, :].astype(F32)
-        u = w + c.x[NS_ITERS % 2, 2, rows, :].astype(F32)
-        want = jnp.sqrt(jnp.sum(w * w, axis=1, keepdims=True) + norm_epsilon)
-        have = jnp.sqrt(jnp.sum(u * u, axis=1, keepdims=True) + norm_epsilon)
-        c.x[NS_ITERS % 2, 2, rows, :] = (u * (want / have)).astype(BF16)
+        c.want_down[rows, :] = jnp.sqrt(jnp.sum(w * w, axis=1, keepdims=True) + norm_epsilon)
 
     loop(c.width // 128, by_row)
+
+
+def renorm(c):
+    x = c.x.at[NS_ITERS % 2]
+    for m, ref in ((0, c.wg), (1, c.wu)):
+        for i in range(c.hid_width // CHUNK):
+            cols = slice(i * CHUNK, (i + 1) * CHUNK)
+            u = ref[:, cols].astype(F32) + x[m, :, cols].astype(F32)
+            have = lax.rsqrt(jnp.sum(u * u, axis=0, keepdims=True) + norm_epsilon)
+            x[m, :, cols] = (u * (c.want[m, :, cols] * have)).astype(BF16)
+    for i in range(c.width // 128):
+        rows = slice(i * 128, (i + 1) * 128)
+        u = c.wdt[rows, :].astype(F32) + x[2, rows, :].astype(F32)
+        have = lax.rsqrt(jnp.sum(u * u, axis=1, keepdims=True) + norm_epsilon)
+        x[2, rows, :] = (u * (c.want_down[rows, :] * have)).astype(BF16)
 
 
 def attention(c, first, count):
@@ -198,45 +213,42 @@
     return start + lax.broadcasted_iota(jnp.int32, shape, 0) < c.bound
 
 
-def fast_old(c, quarter):
-    size, edge = c.quarter, c.high - c.low
-    edge //= 2
-    start = quarter * size
-    c.raw[...] = old_rows(c, start, size)
-    finish_rows(c, start, c.raw[: size - edge, :])
-
-    @pl.when(quarter == 0)
-    def _():
-        finish_rows(c, start + size - edge, c.raw[size - edge :, :])
-
-    @pl.when(quarter == 1)
-    def _():
-        c.open_raw[...] = c.raw[size - edge :, :]
+def fast_old(c, block):
+    size = c.rows // 2
+    start = block * c.rows
+    c.raw[...] = old_rows(c, start, c.rows)
+    finish_rows(c, start, c.raw[:size, :])
+
+    @pl.when(start + c.rows <= c.low)
+    def _():
+        finish_rows(c, start + size, c.raw[size:, :])
+
+    @pl.when(start + c.rows > c.low)
+    def _():
+        c.open_raw[...] = c.raw[size:, :]
 
 
 def close_edge(c):
-    edge = (c.high - c.low) // 2
-    after = new_rows(c, c.low, edge)
+    after = new_rows(c, c.low, c.rows // 2)
     finish_rows(c, c.low, jnp.where(below_bound(c, c.low, after.shape), c.open_raw[...], after))
 
 
-def fast_new(c, quarter):
-    size, edge = c.quarter, (c.high - c.low) // 2
-    start = quarter * size
-    c.raw[...] = new_rows(c, start, size)
-
-    @pl.when(quarter == 2)
-    def _():
-        before = old_rows(c, start, edge)
-        after = c.raw[:edge, :]
-        c.raw[:edge, :] = jnp.where(below_bound(c, start, after.shape), before, after)
+def fast_new(c, block):
+    size = c.rows // 2
+    start = block * c.rows
+    c.raw[...] = new_rows(c, start, c.rows)
+
+    @pl.when(start < c.high)
+    def _():
+        before = old_rows(c, start, size)
+        after = c.raw[:size, :]
+        c.raw[:size, :] = jnp.where(below_bound(c, start, after.shape), before, after)
 
     finish_rows(c, start, c.raw[...])
 
 
 def scratch_of(length, width, hid_width, rows, peers):
     dma = pltpu.SemaphoreType.DMA
-    quarter, edge = length // 4, length // 16
     return {
         "q": pltpu.VMEM((length, width), BF16),
         "k": pltpu.VMEM((WINDOW + length, width), BF16),
@@ -265,12 +277,15 @@
         "target_t": pltpu.VMEM((width, rows), BF16),
         "k_t": pltpu.VMEM((width, rows), BF16),
         "grad": pltpu.VMEM((3, width, hid_width), F32),
+        "squares": pltpu.VMEM((3, 8, hid_width), F32),
+        "want": pltpu.VMEM((2, 1, hid_width), F32),
+        "want_down": pltpu.VMEM((width, 1), F32),
         "x": pltpu.VMEM((2, 3, width, hid_width), BF16),
         "a": pltpu.VMEM((3, width, width), BF16),
         "p": pltpu.VMEM((3, width, width), BF16),
-        "apply_hid": pltpu.VMEM((quarter, hid_width), BF16),
-        "raw": pltpu.VMEM((quarter, width), F32),
-        "open_raw": pltpu.VMEM((edge, width), F32),
+        "apply_hid": pltpu.VMEM((rows, hid_width), BF16),
+        "raw": pltpu.VMEM((rows, width), F32),
+        "open_raw": pltpu.VMEM((rows // 2, width), F32),
         "w_sem": dma((5,)),
     }
 
@@ -278,7 +293,7 @@
 def sizes(length, width, hid_width, rows):
     low, high = length // 2 - length // 16, length // 2 + length // 16
     return dict(
-        length=length, width=width, hid_width=hid_width, rows=rows, low=low, high=high, quarter=length // 4
+        length=length, width=width, hid_width=hid_width, rows=rows, low=low, high=high
     )
 
 
@@ -506,13 +521,14 @@
         copy.wait()
     transpose_down(c)
     clear_gradients(c)
+    measure_start(c)
 
     @pl.when(tok < 2)
     def _():
         c.k[:WINDOW, :] = jnp.zeros((WINDOW, width), BF16)
         c.v[:WINDOW, :] = jnp.zeros((WINDOW, width), BF16)
 
-    tiles = c.quarter // (WINDOW // 2)
+    tiles = rows // (WINDOW // 2)
 
     def got_first_late():
         got_kv(first_late, 1)
@@ -527,16 +543,19 @@
         for halo in halos:
             pl.when(has_after)(halo.start)
 
-    def attend(quarter):
-        for j in range(half):
-            got_q(quarter * half + j)
-
-        @pl.when(quarter == 0)
+    def block_of(quarter, j):
+        return quarter * half + (j + column) % half
+
+    def attend(quarter, j):
+        peer = block_of(quarter, j)
+        got_q(peer)
+
+        @pl.when((quarter == 0) & (j == 0) & has_before)
         def _():
             for halo in halos:
-                pl.when(has_before)(halo.wait_recv)
-
-        attention(c, quarter * tiles, tiles)
+                halo.wait_recv()
+
+        attention(c, peer * tiles, tiles)
 
     def train(i):
         p = flip_by(column, i, group)
@@ -553,16 +572,18 @@
 
             @pl.when(parity == 1)
             def _():
+                @pl.when(side == 1)
+                def _():
+                    for d in along:
+                        q_copy(flip(me, d, peers)).wait_send()
+                    send_corner()
+
                 got_first_late()
                 got_last()
-                attend(3)
-
-                @pl.when(side == 1)
-                def _():
-                    got_q(2 * half)
-                    send_corner()
-                    got_q(2 * half + 1)
-                    attention(c, 2 * tiles, tiles)
+
+        @pl.when((parity == 1) & ((i == half - 1) | ((i == half) & (side == 1))))
+        def _():
+            loop(half, lambda j: attend(half + 2 - i, j))
 
     loop(group, train)
 
@@ -575,67 +596,74 @@
         got_last()
 
     scale_gradients(c)
-
-    def improve(i):
-        sweep(c, i)
-        quarter = 1 - side
-
-        @pl.when((parity == 1) & (i == 0))
-        def _():
-            attend(quarter)
-            fast_old(c, quarter)
-            for j in range(half):
-                pl.when((quarter == 0) | (j < half - 1))(
-                    functools.partial(hand_out, quarter * half + j)
-                )
-
-    loop(NS_ITERS, improve)
+    for turn in range(NS_ITERS):
+        sweep(c, turn)
+
+        if turn == 1:
+
+            @pl.when(parity == 1)
+            def _():
+                def step(j):
+                    peer = block_of(1 - side, j)
+                    attend(1 - side, j)
+                    fast_old(c, peer)
+                    pl.when(peer != group - 1)(functools.partial(hand_out, peer))
+
+                loop(half, step)
+
     renorm(c)
 
-    def last(s):
+    def last(step):
+        s, j = step // half, step % half
         early = jnp.where(side == 0, pick(s, (2, 1, 3, 0)), pick(s, (1, 3, 0, 2)))
         late = pick(s, (3 - side, side, 2 + side))
         quarter = jnp.where(parity == 0, early, late)
 
-        @pl.when((parity == 0) & (s == 1))
+        peer = block_of(quarter, j)
+
+        @pl.when((parity == 0) & (s == 1) & (j == 0))
         def _():
             pl.when(side == 0)(got_last)
             pl.when(side == 1)(got_first_late)
+            send_q(across)
+
+            @pl.when(side == 0)
+            def _():
+                for i in range(half):
+                    hand_out(2 * half + i)
 
         @pl.when((parity == 0) | (s == 1) | ((s == 2) & (side == 0)))
         def _():
-            attend(quarter)
+            attend(quarter, j)
 
         @pl.when(quarter < 2)
         def _():
-            fast_old(c, quarter)
+            fast_old(c, peer)
 
         @pl.when(quarter >= 2)
         def _():
-            fast_new(c, quarter)
-
-        for j in range(half):
-            pl.when((quarter != 1) | (j < half - 1))(
-                functools.partial(hand_out, quarter * half + j)
-            )
-
-        @pl.when((quarter == 1) | ((parity == 1) & (side == 0) & (s == 0)))
+            fast_new(c, peer)
+
+        now = (peer != group - 1) & ((parity == 1) | (side == 1) | (s > 0))
+        pl.when(now)(functools.partial(hand_out, peer))
+        late_edge = (parity == 1) & (side == 0) & (s == 0) & (j == half - 1)
+
+        @pl.when((peer == group - 1) | late_edge)
         def _():
             close_edge(c)
             hand_out(group - 1)
 
-        @pl.when((parity == 0) & (s == 0))
-        def _():
-            send_q(across)
-
-    loop(jnp.where(parity == 0, 4, 3), last)
+    loop(jnp.where(parity == 0, 4, 3) * half, last)
     keep.wait()
     for d in everyone:
         taken(flip(me, d, peers)).wait_recv()
     for d in everyone:
         peer = flip(me, d, peers)
         give(peer).wait_send()
-        q_copy(peer).wait_send()
+        if d in along:
+            pl.when((parity == 0) | (side == 0))(q_copy(peer).wait_send)
+        else:
+            q_copy(peer).wait_send()
         for t in range(2):
             for h in range(2):
                 kv_copy(t, h, peer).wait_send()

time: 112 us -> 102 us (0.911)
  the two profiles are of different devices: /device:TPU:27 before, /device:TPU:0 now
where the time goes in v2:
time: 102 us; the launch traced here: 101 us
  Pallas kernels  98.1 us (96%)
  local copies, waits for them, and re-layouts  3.13 us (3%)
    pallas_call x1, Pallas kernels, body(): pl.pallas_call(functools.partial(kernel, tuple(scratch), sizes(length, wi...  98.1 us
    unnamed x1, local copies, waits for them, and re-layouts  3.13 us

profile of v2, /device:TPU:0, one launch (start us, length us, event | category | flops | bytes accessed | tf_op | source)
XLA Modules:
  0.0 101.2 jit_solution(14817905411058455196)
XLA Ops:
  0.0 98.1 %layer.1 = bf16[256,4096]{1,0:T(8,128)(2,1)} custom-call(s32[4]{0:T(128)} %bounds.1, f32[8,1,512]{2,1,0:T(1,128)} %bitcast.2, bf16[256,4096]{1,0:T(8,128)(2,1)} %q.1, bf16[256,4096]{1,0:T(8,128)(2,1)} %k.1, bf16[256,4096]{1,0:T(8,128)(2,1)} %v.1, bf16[8,256]{1,0:T(8,128)(2,1)} %bitcast.3, bf16[2,512,1024]{2,1,0:T(8,128)(2,1)} %gate_all.1, ...), custom_call_target="tpu_custom_call" | custom-call | tf_op jit(solution)/shard_map/layer/pallas_call | solution.py:687
  98.1 3.1 %copy.11 = bf16[256,4096]{1,0:T(8,128)(2,1)} copy(bf16[256,4096]{1,0:T(8,128)(2,1)} %layer.1) | data formatting | bytes 4194304

commit v3 on v2

--- a/solution.py
+++ b/solution.py
@@ -247,7 +247,7 @@
     finish_rows(c, start, c.raw[...])
 
 
-def scratch_of(length, width, hid_width, rows, peers):
+def scratch_of(length, width, hid_width, rows, peers, segments):
     dma = pltpu.SemaphoreType.DMA
     return {
         "q": pltpu.VMEM((length, width), BF16),
@@ -256,6 +256,7 @@
         "my_rates": pltpu.VMEM((peers, rows), BF16),
         "rates": pltpu.VMEM((peers, peers, rows), BF16),
         "gain": pltpu.VMEM((peers, 1, width), F32),
+        "bounds": pltpu.SMEM(segments, jnp.int32),
         "out": pltpu.VMEM((length, width), BF16),
         "kv_send": dma((2, 2, peers)),
         "kv_recv": dma((2, 2, peers)),
@@ -286,7 +287,7 @@
         "apply_hid": pltpu.VMEM((rows, hid_width), BF16),
         "raw": pltpu.VMEM((rows, width), F32),
         "open_raw": pltpu.VMEM((rows // 2, width), F32),
-        "w_sem": dma((5,)),
+        "w_sem": dma((6,)),
     }
 
 
@@ -361,13 +362,13 @@
     before = ((tok + toks - 2) % toks, column)
     has_after, has_before = tok < toks - 2, tok >= 2
     c.feature = 2 * column + parity
-    c.bound = bounds[tok // 2]
     c.first_segment = jnp.where(tok < 2, 1, 0)
     loads = [
         pltpu.make_async_copy(source, mine, c.w_sem.at[i])
         for i, (source, mine) in enumerate(
             (
                 (r, c.my_rates),
+                (bounds, c.bounds),
                 (gain, c.gain),
                 (gate_all.at[parity], c.wg),
                 (up_all.at[parity], c.wu),
@@ -519,6 +520,7 @@
 
     for copy in loads[1:] + owns:
         copy.wait()
+    c.bound = c.bounds[tok // 2]
     transpose_down(c)
     clear_gradients(c)
     measure_start(c)
@@ -682,23 +684,27 @@
     heads, width, hid_width = token_rates.shape[1], gate_start.shape[1], gate_start.shape[2]
     peers = 2 * group
     length = peers * rows
-    anywhere = pl.BlockSpec(memory_space=pl.ANY)
-    scratch = scratch_of(length, width, hid_width, rows, peers)
+    scratch = scratch_of(length, width, hid_width, rows, peers, bounds.shape)
     return pl.pallas_call(
         functools.partial(
             kernel, tuple(scratch), sizes(length, width, hid_width, rows), group, toks
         ),
         out_shape=jax.ShapeDtypeStruct((rows, feats), BF16),
-        in_specs=[pl.BlockSpec(memory_space=pltpu.SMEM)] + [anywhere] * 8,
-        out_specs=anywhere,
+        in_specs=[pl.BlockSpec(memory_space=pltpu.HBM)] * 9,
+        out_specs=pl.BlockSpec(memory_space=pl.ANY),
         scratch_shapes=list(scratch.values()),
         compiler_params=pltpu.CompilerParams(
-            collective_id=0, has_side_effects=True, vmem_limit_bytes=66000000
+            collective_id=0, has_side_effects=True, vmem_limit_bytes=50000000
         ),
         name="layer",
     )(
-        bounds, norm_gain.reshape(heads, 1, width), queries, keys, values, token_rates.T,
-        gate_start, up_start, down_start,
+        *(
+            pltpu.with_memory_space_constraint(x, pltpu.HBM)
+            for x in (
+                bounds, norm_gain.reshape(heads, 1, width), queries, keys, values, token_rates.T,
+                gate_start, up_start, down_start,
+            )
+        )
     )
 
 

time: 102 us -> 98.8 us (0.969)
  local copies, waits for them, and re-layouts: 3.13 us -> 1.32 us
    unnamed x1, local copies, waits for them, and re-layouts: 3.13 us -> 1.32 us
where the time goes in v3:
time: 98.8 us; the launch traced here: 98.5 us
  Pallas kernels  97.2 us (98%)
  local copies, waits for them, and re-layouts  1.32 us (1%)
    pallas_call x1, Pallas kernels, body(): pl.pallas_call(functools.partial(kernel, tuple(scratch), sizes(length, wi...  97.2 us

profile of v3, /device:TPU:0, one launch (start us, length us, event | category | flops | bytes accessed | tf_op | source)
XLA Modules:
  0.0 98.5 jit_solution(594504342600438911)
XLA Ops:
  0.0 97.2 %layer.1 = bf16[256,4096]{1,0:T(8,128)(2,1)S(1)} custom-call(s32[4]{0:T(128)} %bounds.1, f32[8,1,512]{2,1,0:T(1,128)} %bitcast.2, bf16[256,4096]{1,0:T(8,128)(2,1)} %q.1, bf16[256,4096]{1,0:T(8,128)(2,1)} %k.1, bf16[256,4096]{1,0:T(8,128)(2,1)} %v.1, bf16[8,256]{1,0:T(8,128)(2,1)} %bitcast.3, bf16[2,512,1024]{2,1,0:T(8,128)(2,1)} %gate_all.1, ...), custom_call_target="tpu_custom_call" | custom-call | tf_op jit(solution)/shard_map/layer/pallas_call | solution.py:688
  97.2 1.3 %copy.11 = bf16[256,4096]{1,0:T(8,128)(2,1)} copy(bf16[256,4096]{1,0:T(8,128)(2,1)S(1)} %layer.1) | data formatting | bytes 4194304

commit v4 on v3

--- a/solution.py
+++ b/solution.py
@@ -615,11 +615,23 @@
 
     renorm(c)
 
+    def quarter_at(s):
+        early = jnp.where(side == 0, pick(s, (2, 1, 3, 0)), pick(s, (1, 3, 0, 2)))
+        late = pick(s, (3 - side, side, 2 + side))
+        return jnp.where(parity == 0, early, late)
+
     def last(step):
         s, j = step // half, step % half
-        early = jnp.where(side == 0, pick(s, (2, 1, 3, 0)), pick(s, (1, 3, 0, 2)))
-        late = pick(s, (3 - side, side, 2 + side))
-        quarter = jnp.where(parity == 0, early, late)
+        before = jnp.maximum(step - 1, 0)
+        opened = block_of(quarter_at(before // half), before % half) == group - 1
+        early_edge = (parity == 1) & (side == 0)
+
+        @pl.when(((step > 0) & opened) | ((step == 0) & early_edge))
+        def _():
+            close_edge(c)
+            hand_out(group - 1)
+
+        quarter = quarter_at(s)
 
         peer = block_of(quarter, j)
 
@@ -648,12 +660,6 @@
 
         now = (peer != group - 1) & ((parity == 1) | (side == 1) | (s > 0))
         pl.when(now)(functools.partial(hand_out, peer))
-        late_edge = (parity == 1) & (side == 0) & (s == 0) & (j == half - 1)
-
-        @pl.when((peer == group - 1) | late_edge)
-        def _():
-            close_edge(c)
-            hand_out(group - 1)
 
     loop(jnp.where(parity == 0, 4, 3) * half, last)
     keep.wait()

time: 98.8 us -> 98.7 us (level)
  no operation moved by 1% of the time
where the time goes in v4:
time: 98.7 us; the launch traced here: 98.5 us
  Pallas kernels  97.2 us (98%)
  local copies, waits for them, and re-layouts  1.32 us (1%)
    pallas_call x1, Pallas kernels, body(): pl.pallas_call(functools.partial(kernel, tuple(scratch), sizes(length, wi...  97.2 us

profile of v4, /device:TPU:0, one launch (start us, length us, event | category | flops | bytes accessed | tf_op | source)
XLA Modules:
  0.0 98.5 jit_solution(3087864974059939846)
XLA Ops:
  0.0 97.2 %layer.1 = bf16[256,4096]{1,0:T(8,128)(2,1)S(1)} custom-call(s32[4]{0:T(128)} %bounds.1, f32[8,1,512]{2,1,0:T(1,128)} %bitcast.2, bf16[256,4096]{1,0:T(8,128)(2,1)} %q.1, bf16[256,4096]{1,0:T(8,128)(2,1)} %k.1, bf16[256,4096]{1,0:T(8,128)(2,1)} %v.1, bf16[8,256]{1,0:T(8,128)(2,1)} %bitcast.3, bf16[2,512,1024]{2,1,0:T(8,128)(2,1)} %gate_all.1, ...), custom_call_target="tpu_custom_call" | custom-call | tf_op jit(solution)/shard_map/layer/pallas_call | solution.py:694
  97.2 1.3 %copy.11 = bf16[256,4096]{1,0:T(8,128)(2,1)} copy(bf16[256,4096]{1,0:T(8,128)(2,1)S(1)} %layer.1) | data formatting | bytes 4194304

commit v5 on v4

--- a/solution.py
+++ b/solution.py
@@ -637,9 +637,10 @@
 
         @pl.when((parity == 0) & (s == 1) & (j == 0))
         def _():
+            pl.when(side == 1)(functools.partial(send_q, across))
             pl.when(side == 0)(got_last)
             pl.when(side == 1)(got_first_late)
-            send_q(across)
+            pl.when(side == 0)(functools.partial(send_q, across))
 
             @pl.when(side == 0)
             def _():

time: 98.7 us -> 98.7 us (level)
  no operation moved by 1% of the time
where the time goes in v5:
time: 98.7 us; the launch traced here: 98.5 us
  Pallas kernels  97.2 us (98%)
  local copies, waits for them, and re-layouts  1.32 us (1%)
    pallas_call x1, Pallas kernels, body(): pl.pallas_call(functools.partial(kernel, tuple(scratch), sizes(length, wi...  97.2 us

profile of v5, /device:TPU:0, one launch (start us, length us, event | category | flops | bytes accessed | tf_op | source)
XLA Modules:
  0.0 98.5 jit_solution(12191161763569100745)
XLA Ops:
  0.0 97.2 %layer.1 = bf16[256,4096]{1,0:T(8,128)(2,1)S(1)} custom-call(s32[4]{0:T(128)} %bounds.1, f32[8,1,512]{2,1,0:T(1,128)} %bitcast.2, bf16[256,4096]{1,0:T(8,128)(2,1)} %q.1, bf16[256,4096]{1,0:T(8,128)(2,1)} %k.1, bf16[256,4096]{1,0:T(8,128)(2,1)} %v.1, bf16[8,256]{1,0:T(8,128)(2,1)} %bitcast.3, bf16[2,512,1024]{2,1,0:T(8,128)(2,1)} %gate_all.1, ...), custom_call_target="tpu_custom_call" | custom-call | tf_op jit(solution)/shard_map/layer/pallas_call | solution.py:695
  97.2 1.3 %copy.11 = bf16[256,4096]{1,0:T(8,128)(2,1)} copy(bf16[256,4096]{1,0:T(8,128)(2,1)S(1)} %layer.1) | data formatting | bytes 4194304
